TPU v7x, 256 devices: a whole 4x4x8 slice. The times are simulated.
256 devices in a mesh: section: 8 (over x, y_hi), shard: 32 (over z, y_lo, core).
Axes of the slice: x: 4, y: 4 (y_hi: 2, y_lo: 2; y = y_hi * 2 + y_lo), z: 8, core: 2. Of those that a mesh axis runs over, the one named last changes fastest.
Arguments:
- rows: bfloat16 [8, 2048, 6144], P('section', 'shard'), may hold values from -6 to 6
- expert_ids: int32 [8, 2048, 2], P('section', 'shard'), may hold values from 0 to 7, all different within a row; in each aligned block of 64 rows (0 to 63, 64 to 127, ..., all dimensions but the last counted through in order) at most 18 rows name the same one
- gate_probs: float32 [8, 2048, 2], P('section', 'shard'), may hold values from 0.1 to 1
- w_gate: bfloat16 [8, 6144, 8192], P('section', None, 'shard'), may hold values from -0.078125 to 0.078125
- w_up: bfloat16 [8, 6144, 8192], P('section', None, 'shard'), may hold values from -0.078125 to 0.078125
- w_down: bfloat16 [8, 8192, 6144], P('section', 'shard'), may hold values from -0.0625 to 0.0625
Outputs:
- handed: bfloat16 [8, 2048, 6144], P('section', 'shard')
Inputs may be any that keep to these rules, and one draw needn't show every extreme that they name: `expert_ids`: within each section's block of 64 tokens of one shard index, no expert is named by more than 18 tokens, and each token names 2 different experts.
All inputs are finite; a program needn't handle non-finite values.
Results may differ from a plain program's by a relative error of at most 0.011.
Values may be sent and summed in bfloat16 or wider, within the bound.
A program may use at most 128 MiB of HBM per device.

v0:
```python
import jax
import jax.numpy as jnp
from jax import lax
from jax.sharding import PartitionSpec as P

CAP = 18


def from_behind(value, axis, steps):
    count = lax.axis_size(axis)
    pairs = [(source, (source + steps) % count) for source in range(count)]
    return lax.ppermute(value, axis, pairs)


def unpack_rows(slot_values, expert_out, capacity):
    marks = jnp.arange(capacity, dtype=jnp.float32)[:, None]
    placed = (slot_values[None, :] == marks).astype(jnp.bfloat16)
    return lax.dot_general(
        placed, expert_out, (((0,), (0,)), ((), ())), preferred_element_type=jnp.float32
    )


def on_device(rows, expert_ids, gate_probs, w_gate, w_up, w_down):
    tokens = rows[0]
    chosen_ids = expert_ids[0]
    probs = gate_probs[0]
    gate_w = w_gate[0]
    up_w = w_up[0]
    down_w = w_down[0]
    section_num = lax.axis_index("section")
    hit = chosen_ids == section_num
    routed = jnp.any(hit, axis=-1)
    weight = jnp.sum(jnp.where(hit, probs, jnp.float32(0.0)), axis=-1)
    slot = jnp.cumsum(routed.astype(jnp.int32)) - 1
    slot_values = jnp.where(routed, slot, -1).astype(jnp.float32)
    marks = jnp.arange(CAP, dtype=jnp.float32)[:, None]
    placed = (slot_values[None, :] == marks).astype(jnp.bfloat16)
    packed = jnp.dot(placed, tokens, preferred_element_type=jnp.float32).astype(jnp.bfloat16)
    piece = lax.all_gather(packed, "shard", axis=0, tiled=True)
    gate = jnp.dot(piece, gate_w, preferred_element_type=jnp.float32)
    upper = jnp.dot(piece, up_w, preferred_element_type=jnp.float32)
    hidden_all = (jax.nn.silu(gate) * upper).astype(jnp.bfloat16)
    expert_out = lax.psum_scatter(
        jnp.dot(hidden_all, down_w, preferred_element_type=jnp.float32).astype(jnp.bfloat16),
        "shard",
        scatter_dimension=0,
        tiled=True,
    )
    per_token = unpack_rows(slot_values, expert_out, CAP)
    layer_out = (tokens.astype(jnp.float32) + weight[:, None] * per_token).astype(jnp.bfloat16)
    handed = from_behind(layer_out, "section", 1)
    return handed[None]


def solution(mesh):
    in_specs = (
        P("section", "shard", None),
        P("section", "shard", None),
        P("section", "shard", None),
        P("section", None, "shard"),
        P("section", None, "shard"),
        P("section", "shard", None),
    )
    out_specs = P("section", "shard", None)
    return jax.shard_map(
        on_device, mesh=mesh, in_specs=in_specs, out_specs=out_specs, check_vma=False
    )
```

profile of v0, /device:TPU:40, one launch (start us, length us, event | category | flops | bytes accessed | tf_op | source)
XLA Modules:
  0.0 356.0 jit_solution(13705711673027606384)
XLA Ops:
  7.7 2.1 fusion.3
  9.8 75.4 %all-gather.3.cloned.1.call-done = bf16[32,18,6144]{2,1,0:T(8,128)(2,1)} async-done(((bf16[1,18,6144]{2,1,0:T(8,128)(2,1)}), bf16[32,18,6144]{2,1,0:T(8,128)(2,1)}) %all-gather.3.cloned.1.call-update) | async-done | bytes 7077904 | tf_op jit(solution)/shard_map/all_gather | solution.py:39
  85.3 9.6 %reshape.43 = bf16[576,6144]{1,0:T(8,128)(2,1)} reshape(bf16[32,18,6144]{2,1,0:T(8,128)(2,1)} %all-gather.3.cloned.1.call-done) | data formatting | bytes 14155776
  94.9 6.0 %fusion.7 = f32[576,256]{1,0:T(8,128)S(1)} fusion(bf16[576,6144]{1,0:T(8,128)(2,1)} %reshape.43, bf16[1,6144,256]{2,1,0:T(8,128)(2,1)} %param.9), kind=kOutput, calls=%fused_computation.9 | convolution fusion | flops 1811939328 | bytes 10813440 | tf_op jit(solution)/shard_map/dot_general | solution.py:40
  101.7 2.0 fusion.12
  103.7 4.9 %convolution_convert_fusion = bf16[576,6144]{1,0:T(8,128)(2,1)} fusion(bf16[576,256]{1,0:T(8,128)(2,1)S(1)} %fusion.12, bf16[1,256,6144]{2,1,0:T(8,128)(2,1)S(1)} %copy-done), kind=kOutput, calls=%fused_computation | convolution fusion | flops 1815478272 | bytes 10518528 | tf_op jit(solution)/shard_map/dot_general | solution.py:44
  108.6 108.9 %fusion = bf16[24,6144]{1,0:T(8,128)(2,1)S(1)} fusion(bf16[576,6144]{1,0:T(8,128)(2,1)} %convolution_convert_fusion), kind=kCustom, calls=%all-reduce-scatter | all-reduce-scatter fusion | flops 4718593 | bytes 7373824
  217.5 1.9 collective-permute-start.1
  219.4 1.9 collective-permute-start.2
  221.4 3.0 collective-permute-start.8
  224.5 3.5 collective-permute-start.3
  228.0 3.1 collective-permute-start.4
  231.1 10.0 %collective-permute-done.8 = bf16[18,6144]{1,0:T(8,128)(2,1)S(1)} collective-permute-done((bf16[18,6144]{1,0:T(8,128)(2,1)S(1)}, bf16[18,6144]{1,0:T(8,128)(2,1)S(1)}, u32[]{:S(2)}, u32[]{:S(2)}) %collective-permute-start.8) | collective-permute-done | bytes 221216
  241.1 3.7 %collective-permute-start.5 = (bf16[24,6144]{1,0:T(8,128)(2,1)S(1)}, bf16[24,6144]{1,0:T(8,128)(2,1)}, u32[]{:S(2)}, u32[]{:S(2)}) collective-permute-start(bf16[24,6144]{1,0:T(8,128)(2,1)S(1)} %fusion), channel_id=1, source_target_pairs={{0,5},{1,6},{2,7},{3,8},{4,9},{5,10},{6,11},{7,12},{8,13},{9,14},{... | collective-permute-start | bytes 884744
  244.8 1.9 collective-permute-start.6
  246.8 7.8 %collective-permute-start.7 = (bf16[24,6144]{1,0:T(8,128)(2,1)S(1)}, bf16[24,6144]{1,0:T(8,128)(2,1)}, u32[]{:S(2)}, u32[]{:S(2)}) collective-permute-start(bf16[24,6144]{1,0:T(8,128)(2,1)S(1)} %fusion), channel_id=1, source_target_pairs={{0,7},{1,8},{2,9},{3,10},{4,11},{5,12},{6,13},{7,14},{8,15},{9,16}... | collective-permute-start | bytes 884744
  256.0 13.5 %collective-permute-done.4 = bf16[24,6144]{1,0:T(8,128)(2,1)} collective-permute-done((bf16[24,6144]{1,0:T(8,128)(2,1)S(1)}, bf16[24,6144]{1,0:T(8,128)(2,1)}, u32[]{:S(2)}, u32[]{:S(2)}) %collective-permute-start.4) | collective-permute-done | bytes 294944
  269.5 6.3 %collective-permute-done.5 = bf16[24,6144]{1,0:T(8,128)(2,1)} collective-permute-done((bf16[24,6144]{1,0:T(8,128)(2,1)S(1)}, bf16[24,6144]{1,0:T(8,128)(2,1)}, u32[]{:S(2)}, u32[]{:S(2)}) %collective-permute-start.5) | collective-permute-done | bytes 294944
  275.9 6.3 %collective-permute-done.6 = bf16[24,6144]{1,0:T(8,128)(2,1)} collective-permute-done((bf16[24,6144]{1,0:T(8,128)(2,1)S(1)}, bf16[24,6144]{1,0:T(8,128)(2,1)}, u32[]{:S(2)}, u32[]{:S(2)}) %collective-permute-start.6) | collective-permute-done | bytes 294944
  282.2 6.3 %collective-permute-done.7 = bf16[24,6144]{1,0:T(8,128)(2,1)} collective-permute-done((bf16[24,6144]{1,0:T(8,128)(2,1)S(1)}, bf16[24,6144]{1,0:T(8,128)(2,1)}, u32[]{:S(2)}, u32[]{:S(2)}) %collective-permute-start.7) | collective-permute-done | bytes 294944
  288.5 34.5 %concatenate = bf16[210,6144]{1,0:T(8,128)(2,1)} concatenate(bf16[18,6144]{1,0:T(8,128)(2,1)} %copy-done.4, bf16[24,6144]{1,0:T(8,128)(2,1)} %collective-permute-done.7, bf16[24,6144]{1,0:T(8,128)(2,1)} %collective-permute-done.6, bf16[24,6144]{1,0:T(8,128)(2,1)} %collective-permute-done.5, bf16[24,6144]{1,0:T(8,128)(2,1)} %collective-permute-done.4, ...), dimensions={0} | concatenate | bytes 5160960
  323.0 1.7 fusion.2
  324.7 2.2 collective-permute-start
  326.9 21.4 %collective-permute-done = bf16[64,6144]{1,0:T(8,128)(2,1)S(1)} collective-permute-done((bf16[64,6144]{1,0:T(8,128)(2,1)S(1)}, bf16[64,6144]{1,0:T(8,128)(2,1)S(1)}, u32[]{:S(2)}, u32[]{:S(2)}) %collective-permute-start) | collective-permute-done | bytes 786464 | tf_op jit(solution)/shard_map/ppermute | solution.py:12
  (33 shorter events, 3.6 us)
Async XLA Ops:
  6.5 97.1 %copy-start = (bf16[1,256,6144]{2,1,0:T(8,128)(2,1)S(1)}, bf16[1,256,6144]{2,1,0:T(8,128)(2,1)}, u32[]{:S(2)}) copy-start(bf16[1,256,6144]{2,1,0:T(8,128)(2,1)} %param.11) | copy-start | bytes 9437188
  6.5 78.7 %all-gather.3.cloned.1.call-start = ((), (), s32[]{:S(2)}) async-start(), calls=%async_computation | async-start | bytes 9732096 | tf_op jit(solution)/shard_map/all_gather | solution.py:39
  94.8 6.1 %copy-start.1 = (bf16[576,6144]{1,0:T(8,128)(2,1)S(1)}, bf16[576,6144]{1,0:T(8,128)(2,1)}, u32[]{:S(2)}) copy-start(bf16[576,6144]{1,0:T(8,128)(2,1)} %reshape.43) | copy-start | bytes 21233668
  94.8 6.8 %copy-start.8 = (bf16[1,6144,256]{2,1,0:T(8,128)(2,1)S(1)}, bf16[1,6144,256]{2,1,0:T(8,128)(2,1)}, u32[]{:S(2)}) copy-start(bf16[1,6144,256]{2,1,0:T(8,128)(2,1)} %param.10) | copy-start | bytes 9437188
  108.6 146.0 %copy-start.7 = (u32[256]{0:T(256)S(1)}, u32[256]{0:T(256)}, u32[]{:S(2)}) copy-start(u32[256]{0:T(256)} %constant.29) | copy-start | bytes 3076
  108.6 147.4 %copy-start.5 = (s32[1,64,2]{1,2,0:T(2,128)S(1)}, s32[1,64,2]{1,2,0:T(2,128)}, u32[]{:S(2)}) copy-start(s32[1,64,2]{1,2,0:T(2,128)} %param.7) | copy-start | bytes 1540
  108.6 147.4 %copy-start.6 = (f32[1,64,2]{1,2,0:T(2,128)S(1)}, f32[1,64,2]{1,2,0:T(2,128)}, u32[]{:S(2)}) copy-start(f32[1,64,2]{1,2,0:T(2,128)} %param.8) | copy-start | bytes 1540
  217.5 27.3 %collective-permute-start.1 = (bf16[24,6144]{1,0:T(8,128)(2,1)S(1)}, bf16[24,6144]{1,0:T(8,128)(2,1)S(1)}, u32[]{:S(2)}, u32[]{:S(2)}) collective-permute-start(bf16[24,6144]{1,0:T(8,128)(2,1)S(1)} %fusion), channel_id=1, source_target_pairs={{0,1},{1,2},{2,3},{3,4},{4,5},{5,6},{6,7},{7,8},{8,9},{9,10},{10,1... | collective-permute-start | bytes 884744
  219.4 27.3 %collective-permute-start.2 = (bf16[24,6144]{1,0:T(8,128)(2,1)S(1)}, bf16[24,6144]{1,0:T(8,128)(2,1)S(1)}, u32[]{:S(2)}, u32[]{:S(2)}) collective-permute-start(bf16[24,6144]{1,0:T(8,128)(2,1)S(1)} %fusion), channel_id=1, source_target_pairs={{0,2},{1,3},{2,4},{3,5},{4,6},{5,7},{6,8},{7,9},{8,10},{9,11},{10,... | collective-permute-start | bytes 884744
  221.4 19.7 %collective-permute-start.8 = (bf16[18,6144]{1,0:T(8,128)(2,1)S(1)}, bf16[18,6144]{1,0:T(8,128)(2,1)S(1)}, u32[]{:S(2)}, u32[]{:S(2)}) collective-permute-start(bf16[18,6144]{1,0:T(8,128)(2,1)S(1)} %slice), channel_id=1, source_target_pairs={{0,8},{1,9},{2,10},{3,11},{4,12},{5,13},{6,14},{7,15},{8,16},{9,17... | collective-permute-start | bytes 663560
  224.5 31.5 %collective-permute-start.3 = (bf16[24,6144]{1,0:T(8,128)(2,1)S(1)}, bf16[24,6144]{1,0:T(8,128)(2,1)}, u32[]{:S(2)}, u32[]{:S(2)}) collective-permute-start(bf16[24,6144]{1,0:T(8,128)(2,1)S(1)} %fusion), channel_id=1, source_target_pairs={{0,3},{1,4},{2,5},{3,6},{4,7},{5,8},{6,9},{7,10},{8,11},{9,12},{10... | collective-permute-start | bytes 884744
  228.0 41.5 %collective-permute-start.4 = (bf16[24,6144]{1,0:T(8,128)(2,1)S(1)}, bf16[24,6144]{1,0:T(8,128)(2,1)}, u32[]{:S(2)}, u32[]{:S(2)}) collective-permute-start(bf16[24,6144]{1,0:T(8,128)(2,1)S(1)} %fusion), channel_id=1, source_target_pairs={{0,4},{1,5},{2,6},{3,7},{4,8},{5,9},{6,10},{7,11},{8,12},{9,13},{1... | collective-permute-start | bytes 884744
  241.1 13.5 %copy-start.4 = (bf16[18,6144]{1,0:T(8,128)(2,1)}, bf16[18,6144]{1,0:T(8,128)(2,1)S(1)}, u32[]{:S(2)}) copy-start(bf16[18,6144]{1,0:T(8,128)(2,1)S(1)} %collective-permute-done.8) | copy-start | bytes 663556
  241.1 34.8 %collective-permute-start.5 = (bf16[24,6144]{1,0:T(8,128)(2,1)S(1)}, bf16[24,6144]{1,0:T(8,128)(2,1)}, u32[]{:S(2)}, u32[]{:S(2)}) collective-permute-start(bf16[24,6144]{1,0:T(8,128)(2,1)S(1)} %fusion), channel_id=1, source_target_pairs={{0,5},{1,6},{2,7},{3,8},{4,9},{5,10},{6,11},{7,12},{8,13},{9,14},{... | collective-permute-start | bytes 884744
  244.8 2.0 copy-start.2
  244.8 37.4 %collective-permute-start.6 = (bf16[24,6144]{1,0:T(8,128)(2,1)S(1)}, bf16[24,6144]{1,0:T(8,128)(2,1)}, u32[]{:S(2)}, u32[]{:S(2)}) collective-permute-start(bf16[24,6144]{1,0:T(8,128)(2,1)S(1)} %fusion), channel_id=1, source_target_pairs={{0,6},{1,7},{2,8},{3,9},{4,10},{5,11},{6,12},{7,13},{8,14},{9,15},... | collective-permute-start | bytes 884744
  246.7 7.8 %copy-start.3 = (bf16[24,6144]{1,0:T(8,128)(2,1)}, bf16[24,6144]{1,0:T(8,128)(2,1)S(1)}, u32[]{:S(2)}) copy-start(bf16[24,6144]{1,0:T(8,128)(2,1)S(1)} %collective-permute-done.2) | copy-start | bytes 884740
  246.8 41.7 %collective-permute-start.7 = (bf16[24,6144]{1,0:T(8,128)(2,1)S(1)}, bf16[24,6144]{1,0:T(8,128)(2,1)}, u32[]{:S(2)}, u32[]{:S(2)}) collective-permute-start(bf16[24,6144]{1,0:T(8,128)(2,1)S(1)} %fusion), channel_id=1, source_target_pairs={{0,7},{1,8},{2,9},{3,10},{4,11},{5,12},{6,13},{7,14},{8,15},{9,16}... | collective-permute-start | bytes 884744
  324.7 23.6 %collective-permute-start = (bf16[64,6144]{1,0:T(8,128)(2,1)S(1)}, bf16[64,6144]{1,0:T(8,128)(2,1)S(1)}, u32[]{:S(2)}, u32[]{:S(2)}) collective-permute-start(bf16[64,6144]{1,0:T(8,128)(2,1)S(1)} %fusion.2), channel_id=1, source_target_pairs={{0,32},{32,64},{64,96},{96,128},{128,160},{160,192},{192,224},{224... | collective-permute-start | bytes 2359304 | tf_op jit(solution)/shard_map/ppermute | solution.py:12
Sparse Core Ops, SparseCore 0:
  9.9 75.2 all-gather.2
where the time goes:
time: 359 us; the launch traced here: 356 us
  waiting for transfers between devices  139 us (39%)
  blocking collectives  109 us (30%)
  local copies, waits for them, and re-layouts  46.6 us (13%)
  starting transfers between devices  29.1 us (8%)
  matrix products  16.7 us (5%)
  between operations  14.3 us (4%)
    unnamed x1, blocking collectives  109 us
    all_gather x1, waiting for transfers between devices, on_device(): piece = lax.all_gather(packed, 'shard', axis=0, tiled=True)  75.4 us
    unnamed x23, local copies, waits for them, and re-layouts  46.5 us
    unnamed x9, waiting for transfers between devices  42.5 us
    unnamed x8, starting transfers between devices  26.9 us
    ppermute x1, waiting for transfers between devices, from_behind(): return lax.ppermute(value, axis, pairs)  21.4 us
  transfers between devices with their start and end apart: 10, of which 7 were waited for; matrix products, arithmetic and copies ran while one was open for 0% of the time, Pallas kernels for 0%

commit v1 on v0

v1 whole, which is shorter than its diff:
```python
import functools

import jax
import jax.numpy as jnp
from jax import lax
from jax.experimental import pallas as pl
from jax.experimental.pallas import tpu as pltpu
from jax.sharding import PartitionSpec as P

F32 = jnp.float32
BF16 = jnp.bfloat16
MAIN = 16
EXTRA = 2
FOLD = MAIN // EXTRA
MESH = pl.DeviceIdType.MESH


class Chunk:
    def __init__(self, pair, folded, start, width, turn, offset):
        self.pair = pair
        self.folded = folded
        self.cols = pl.ds(start, width)
        self.start = start
        self.width = width
        self.turn = turn
        self.room = pl.ds(offset, width)


def plan(depth):
    unit = depth // 8
    singles = [Chunk(False, True, 0, unit, 1, 0), Chunk(False, False, 0, unit, -1, unit)]
    rest = (depth - unit) // 256
    count = 4 if rest >= 4 else 2
    pairs, at, offset = [], unit, 0
    for i in range(count):
        width = (rest // count + (1 if i < rest % count else 0)) * 256
        if i == count - 1:
            width = depth - at
        pairs.append(Chunk(True, False, at, width, 1 if i % 2 == 0 else -1, offset))
        at += width
        offset += width
    return singles, pairs


def iota(shape, dim):
    return lax.broadcasted_iota(jnp.int32, shape, dim)


def dot(a, b):
    return jnp.dot(a, b, preferred_element_type=F32)


def kernel(
    singles,
    pairs,
    rings,
    rows_hbm,
    ids_ref,
    probs_ref,
    wg_hbm,
    wu_hbm,
    wd_hbm,
    out_ref,
    rows_v,
    rows_p,
    wg,
    wu,
    wd,
    xg,
    xt,
    gacc,
    uacc,
    hid,
    part,
    pt,
    ring_pair,
    ring_one,
    cross_pair,
    cross_one,
    fin,
    eo_s,
    eot_s,
    eo_p,
    eot_p,
    meta_s,
    meta_p,
    send_sem,
    recv_sem,
    local_sem,
):
    tok, depth = rows_v.shape
    units = wg.shape[2]
    fold = depth // FOLD
    total = gacc.shape[0]
    section = lax.axis_index("section")
    sections = lax.axis_size("section")
    me = lax.axis_index("shard")
    core = lax.rem(me, 2)
    y = lax.rem(me // 2, 2)
    z = me // 4
    other = 1 - y

    def at_z(step):
        return lax.rem(z + step + rings, rings)

    def shard_of(zz, yy, cc):
        return {"shard": zz * 4 + yy * 2 + cc}

    following = {"section": lax.rem(section + 1, sections)}
    previous = {"section": lax.rem(section + sections - 1, sections)}
    across = shard_of(z, other, core)
    sibling = shard_of(z, y, 1 - core)
    up_z = shard_of(at_z(1), y, core)
    down_z = shard_of(at_z(-1), y, core)
    far = rings // 2
    hops = {1: far, -1: far - 1}

    used = []
    started = []

    def remote(src, dst, device):
        i = len(used)
        used.append(i)
        copy = pltpu.make_async_remote_copy(
            src_ref=src,
            dst_ref=dst,
            send_sem=send_sem.at[i],
            recv_sem=recv_sem.at[i],
            device_id=device,
            device_id_type=MESH,
        )
        copy.start()
        started.append(copy)
        return copy

    rows_in = pltpu.make_async_copy(rows_hbm.at[0], rows_v, local_sem.at[0])
    rows_in.start()
    own = [
        pltpu.make_async_copy(wg_hbm.at[0], wg.at[0], local_sem.at[1]),
        pltpu.make_async_copy(wu_hbm.at[0], wu.at[0], local_sem.at[2]),
        pltpu.make_async_copy(wd_hbm.at[0], wd.at[pl.ds(0, units)], local_sem.at[3]),
    ]
    for copy in own:
        copy.start()

    barrier = pltpu.get_barrier_semaphore()
    for device in (up_z, down_z, across, sibling, previous):
        pl.semaphore_signal(barrier, inc=1, device_id=device, device_id_type=MESH)

    hit = ids_ref[...] == section
    routed = jnp.max(jnp.where(hit, 1.0, 0.0).astype(F32), axis=0, keepdims=True)
    weight = jnp.sum(jnp.where(hit, probs_ref[...], 0.0), axis=0, keepdims=True)
    upper = (iota((tok, tok), 0) <= iota((tok, tok), 1)).astype(F32)
    count = dot(jnp.broadcast_to(routed, (8, tok)).astype(BF16), upper.astype(BF16))
    slot = jnp.where(routed > 0, count[0:1] - 1.0, -1.0)
    meta_s[...] = jnp.zeros_like(meta_s)
    meta_s[0:1, 0:tok] = slot
    meta_s[1:2, 0:tok] = weight
    place = iota((MAIN, tok), 0).astype(F32)
    placed = jnp.where(slot == place, 1.0, 0.0).astype(BF16)
    row16 = iota((MAIN, tok), 0)
    row_of = (MAIN + row16 // FOLD).astype(F32)

    rows_in.wait()
    pl.semaphore_wait(barrier, 5)

    weights = [
        remote(wg_hbm.at[0], wg.at[1], sibling),
        remote(wu_hbm.at[0], wu.at[1], sibling),
        remote(wd_hbm.at[0], wd.at[pl.ds(units, units)], sibling),
    ]

    def gathered(chunk):
        return xt if chunk.folded else xg

    ring = {}
    cross = {}

    def send_ring(chunk, hop):
        ref = gathered(chunk)
        for turn in (chunk.turn, -chunk.turn):
            if hop > hops[turn * chunk.turn]:
                continue
            held = at_z(-turn * (hop - 1))
            if chunk.pair:
                block = ref.at[:, held, :, chunk.cols]
            else:
                block = ref.at[y, held, :, chunk.cols]
            ring[chunk, turn, hop] = remote(block, block, up_z if turn == 1 else down_z)

    def send_across(chunk, held, key):
        block = gathered(chunk).at[y, held, :, chunk.cols]
        cross[chunk, key] = remote(block, block, across)

    for chunk in singles:
        if chunk.folded:
            folded = jnp.zeros((MAIN, fold), F32)
            for b in range(FOLD):
                pick = jnp.where((slot == row_of) & (row16 % FOLD == b), 1.0, 0.0)
                folded += dot(pick.astype(BF16), rows_v[:, b * fold : (b + 1) * fold])
            xt[y, z] = folded.astype(BF16)
        else:
            xg[y, z, :, chunk.cols] = dot(placed, rows_v[:, chunk.cols]).astype(BF16)
        send_ring(chunk, 1)
    for chunk in pairs:
        xg[y, z, :, chunk.cols] = dot(placed, rows_v[:, chunk.cols]).astype(BF16)
        send_across(chunk, z, 0)
    for chunk in singles:
        send_across(chunk, z, 0)
    for chunk in pairs:
        cross[chunk, 0].wait_recv()
        send_ring(chunk, 1)
    handed = [
        remote(rows_hbm.at[0], rows_p, following),
        remote(meta_s, meta_p, following),
    ]
    for hop in range(1, far + 1):
        for chunk in singles + pairs:
            for turn in (chunk.turn, -chunk.turn):
                if hop > hops[turn * chunk.turn]:
                    continue
                if hop == far and chunk.pair:
                    continue
                ring[chunk, turn, hop].wait_recv()
                if not chunk.pair:
                    send_across(chunk, at_z(-turn * hop), turn * hop)
            if hop < far:
                send_ring(chunk, hop + 1)

    for copy in own[:2]:
        copy.wait()
    for copy in weights[:2]:
        copy.wait_recv()

    def await_single(chunk):
        for key in list(cross):
            if key[0] is chunk:
                cross[key].wait_recv()

    def products(chunk, first):
        for i in range(2):
            to = pl.ds(i * units, units)
            for acc, w in ((gacc, wg), (uacc, wu)):
                x = xg[:, :, :, chunk.cols].reshape(total, chunk.width)
                made = dot(x, w[i, chunk.cols, :])
                if first:
                    acc[:, to] = made
                else:
                    acc[:, to] += made

    await_single(singles[0])
    lane = iota((MAIN, rings * MAIN), 1)
    line = iota((MAIN, rings * MAIN), 0)
    home = (line // EXTRA) * MAIN + (line % EXTRA) * FOLD
    for yy in range(2):
        block = xt[yy].reshape(rings * MAIN, fold)
        for b in range(FOLD):
            pick = jnp.where(lane == home + b, 1.0, 0.0).astype(BF16)
            xg[yy, rings, :, b * fold : (b + 1) * fold] = dot(pick, block).astype(BF16)
    await_single(singles[1])
    products(singles[1], True)
    for chunk in pairs:
        ring[chunk, chunk.turn, far].wait_recv()
        products(chunk, False)

    rows_at_once = 2 * MAIN
    for r in range(0, total, rows_at_once):
        g = gacc[r : r + rows_at_once, :]
        u = uacc[r : r + rows_at_once, :]
        hid[r : r + rows_at_once, :] = (g / (1.0 + jnp.exp(-g)) * u).astype(BF16)

    own[2].wait()
    weights[2].wait_recv()

    def down(chunk):
        step = 256
        for c in range(chunk.start, chunk.start + chunk.width, step):
            c1 = min(c + step, chunk.start + chunk.width)
            made = dot(hid[...], wd[:, c:c1]).astype(BF16)
            part[:, :, :, c:c1] = made.reshape(2, rings + 1, MAIN, c1 - c)

    def partial(chunk):
        return pt if chunk.folded else part

    sums = {}

    def slots(chunk):
        return ring_pair if chunk.pair else ring_one

    def index_of(chunk, turn, hop):
        return hop - 1 if turn == chunk.turn else far + hop - 1

    def send_sum(chunk, hop):
        ref = partial(chunk)
        for turn in (chunk.turn, -chunk.turn):
            last = hops[turn * chunk.turn]
            if hop > last:
                continue
            goal = at_z(turn * (last - hop + 1))
            i = index_of(chunk, turn, hop)
            if chunk.pair:
                src = ref.at[:, goal, :, chunk.cols]
                if hop > 1:
                    before = slots(chunk)[i - 1, :, :, chunk.room]
                    mine = ref[:, goal, :, chunk.cols]
                    ref[:, goal, :, chunk.cols] = (
                        mine.astype(F32) + before.astype(F32)
                    ).astype(BF16)
                dst = slots(chunk).at[i, :, :, chunk.room]
            else:
                src = ref.at[y, goal, :, chunk.cols]
                if hop > 1:
                    before = slots(chunk)[i - 1, :, chunk.room]
                    mine = ref[y, goal, :, chunk.cols]
                    ref[y, goal, :, chunk.cols] = (
                        mine.astype(F32) + before.astype(F32)
                    ).astype(BF16)
                dst = slots(chunk).at[i, :, chunk.room]
            sums[chunk, turn, hop] = remote(src, dst, up_z if turn == 1 else down_z)

    crossed = {}

    def cross_single(chunk):
        block = partial(chunk).at[other, pl.ds(0, rings), :, chunk.cols]
        crossed[chunk] = remote(block, cross_one.at[:, :, chunk.room], across)

    down(singles[1])
    cross_single(singles[1])
    for chunk in pairs:
        down(chunk)
        send_sum(chunk, 1)
    spot = iota((rings * MAIN, MAIN), 0)
    line = iota((rings * MAIN, MAIN), 1)
    home = (line // EXTRA) * MAIN + (line % EXTRA) * FOLD
    for yy in range(2):
        block = jnp.zeros((rings * MAIN, fold), F32)
        for b in range(FOLD):
            pick = jnp.where(spot == home + b, 1.0, 0.0).astype(BF16)
            block += dot(pick, part[yy, rings, :, b * fold : (b + 1) * fold])
        pt[yy] = block.astype(BF16).reshape(rings, MAIN, fold)
    cross_single(singles[0])
    for chunk in (singles[1], singles[0]):
        crossed[chunk].wait_recv()
        ref = partial(chunk)
        for zz in range(rings):
            ref[y, zz, :, chunk.cols] = (
                ref[y, zz, :, chunk.cols].astype(F32)
                + cross_one[zz, :, chunk.room].astype(F32)
            ).astype(BF16)
        send_sum(chunk, 1)
    for hop in range(2, far + 1):
        for chunk in pairs + [singles[1], singles[0]]:
            for turn in (chunk.turn, -chunk.turn):
                if (chunk, turn, hop - 1) in sums:
                    if hop - 1 < hops[turn * chunk.turn]:
                        sums[chunk, turn, hop - 1].wait_recv()
            send_sum(chunk, hop)

    arrive = []

    def finish(chunk):
        for turn in (chunk.turn, -chunk.turn):
            sums[chunk, turn, hops[turn * chunk.turn]].wait_recv()
        ends = [
            index_of(chunk, chunk.turn, hops[1]),
            index_of(chunk, -chunk.turn, hops[-1]),
        ]
        return ends

    def pass_on(chunk):
        if chunk.folded:
            arrive.append(remote(eot_s, eot_p, following))
        else:
            block = eo_s.at[:, chunk.cols]
            arrive.append(remote(block, eo_p.at[:, chunk.cols], following))

    for chunk in pairs:
        ends = finish(chunk)
        for yy, keep in ((other, False), (y, True)):
            made = part[yy, z, :, chunk.cols].astype(F32)
            for i in ends:
                made += ring_pair[i, yy, :, chunk.room].astype(F32)
            if keep:
                fin[:, chunk.room] = made
            else:
                part[yy, z, :, chunk.cols] = made.astype(BF16)
                block = part.at[yy, z, :, chunk.cols]
                crossed[chunk] = remote(block, cross_pair.at[:, chunk.room], across)
    for chunk in (singles[1], singles[0]):
        ends = finish(chunk)
        made = partial(chunk)[y, z, :, chunk.cols].astype(F32)
        for i in ends:
            made += ring_one[i, :, chunk.room].astype(F32)
        if chunk.folded:
            eot_s[...] = made.astype(BF16)
        else:
            eo_s[:, chunk.cols] = made.astype(BF16)
        pass_on(chunk)
    for chunk in pairs:
        crossed[chunk].wait_recv()
        made = fin[:, chunk.room] + cross_pair[:, chunk.room].astype(F32)
        eo_s[:, chunk.cols] = made.astype(BF16)
        pass_on(chunk)

    for copy in handed:
        copy.wait_recv()
    diagonal = iota((tok, tok), 0) == iota((tok, tok), 1)

    def upright(i):
        line = jnp.broadcast_to(meta_p[i : i + 1, 0:tok], (tok, tok))
        return jnp.sum(jnp.where(diagonal, line, 0.0), axis=1, keepdims=True)

    slot_p = upright(0)
    weight_p = upright(1)
    spot = iota((tok, MAIN), 1)
    taken = jnp.where(slot_p == spot.astype(F32), 1.0, 0.0).astype(BF16)
    extra_of = (MAIN + spot // FOLD).astype(F32)
    for copy in arrive[:2]:
        copy.wait_recv()
    for b in range(FOLD):
        at = pl.ds(b * fold, fold)
        for copy, chunk in zip(arrive[2:], pairs):
            begins = chunk.start
            if b * fold <= begins < (b + 1) * fold:
                copy.wait_recv()
        pick = jnp.where((slot_p == extra_of) & (spot % FOLD == b), 1.0, 0.0)
        added = dot(taken, eo_p[:, at]) + dot(pick.astype(BF16), eot_p[...])
        out_ref[0, :, at] = (rows_p[:, at].astype(F32) + weight_p * added).astype(BF16)

    for copy in started:
        copy.wait_send()


def on_device(rows, expert_ids, gate_probs, w_gate, w_up, w_down):
    _, tok, depth = rows.shape
    units = w_gate.shape[2]
    rings = lax.axis_size("shard") // 4
    singles, pairs = plan(depth)
    fold = depth // FOLD
    total = 2 * (rings + 1) * MAIN
    wide = sum(c.width for c in pairs)
    thin = sum(c.width for c in singles)
    steps = rings - 1
    copies = 5
    copies += len(singles) * (steps + rings) + len(pairs) * (steps + 1)
    copies += len(singles) * (steps + 1) + len(pairs) * (steps + 1)
    copies += len(singles) + len(pairs)
    ids = jnp.transpose(expert_ids[0])
    probs = jnp.transpose(gate_probs[0])
    hbm = pl.BlockSpec(memory_space=pltpu.MemorySpace.HBM)
    vmem = pl.BlockSpec(memory_space=pltpu.MemorySpace.VMEM)
    return pl.pallas_call(
        functools.partial(kernel, singles, pairs, rings),
        out_shape=jax.ShapeDtypeStruct(rows.shape, BF16),
        in_specs=[hbm, vmem, vmem, hbm, hbm, hbm],
        out_specs=vmem,
        scratch_shapes=[
            pltpu.VMEM((tok, depth), BF16),
            pltpu.VMEM((tok, depth), BF16),
            pltpu.VMEM((2, depth, units), BF16),
            pltpu.VMEM((2, depth, units), BF16),
            pltpu.VMEM((2 * units, depth), BF16),
            pltpu.VMEM((2, rings + 1, MAIN, depth), BF16),
            pltpu.VMEM((2, rings, MAIN, fold), BF16),
            pltpu.VMEM((total, 2 * units), F32),
            pltpu.VMEM((total, 2 * units), F32),
            pltpu.VMEM((total, 2 * units), BF16),
            pltpu.VMEM((2, rings + 1, MAIN, depth), BF16),
            pltpu.VMEM((2, rings, MAIN, fold), BF16),
            pltpu.VMEM((steps, 2, MAIN, wide), BF16),
            pltpu.VMEM((steps, MAIN, thin), BF16),
            pltpu.VMEM((MAIN, wide), BF16),
            pltpu.VMEM((rings, MAIN, thin), BF16),
            pltpu.VMEM((MAIN, wide), F32),
            pltpu.VMEM((MAIN, depth), BF16),
            pltpu.VMEM((MAIN, fold), BF16),
            pltpu.VMEM((MAIN, depth), BF16),
            pltpu.VMEM((MAIN, fold), BF16),
            pltpu.VMEM((8, 128), F32),
            pltpu.VMEM((8, 128), F32),
            pltpu.SemaphoreType.DMA((copies,)),
            pltpu.SemaphoreType.DMA((copies,)),
            pltpu.SemaphoreType.DMA((4,)),
        ],
        compiler_params=pltpu.CompilerParams(
            collective_id=0, has_side_effects=True, vmem_limit_bytes=56 << 20
        ),
    )(rows, ids, probs, w_gate, w_up, w_down)


def solution(mesh):
    in_specs = (
        P("section", "shard", None),
        P("section", "shard", None),
        P("section", "shard", None),
        P("section", None, "shard"),
        P("section", None, "shard"),
        P("section", "shard", None),
    )
    out_specs = P("section", "shard", None)
    return jax.shard_map(
        on_device, mesh=mesh, in_specs=in_specs, out_specs=out_specs, check_vma=False
    )
```

time: 359 us -> 98.6 us (0.27)
  the two profiles are of different devices: /device:TPU:40 before, /device:TPU:8 now
where the time goes in v1:
time: 98.6 us; the launch traced here: 98.4 us
  Pallas kernels  96.4 us (98%)
  local copies, waits for them, and re-layouts  2.06 us (2%)
    pallas_call x1, Pallas kernels, on_device(): pl.pallas_call(functools.partial(kernel, singles, pairs, rings), out_shap...  96.4 us
    unnamed x1, local copies, waits for them, and re-layouts  2.06 us

profile of v1, /device:TPU:8, one launch (start us, length us, event | category | flops | bytes accessed | tf_op | source)
XLA Modules:
  0.0 98.4 jit_solution(8820445255845507977)
XLA Ops:
  0.0 96.4 %shard_map.64 = bf16[1,64,6144]{2,1,0:T(8,128)(2,1)} custom-call(bf16[1,64,6144]{2,1,0:T(8,128)(2,1)} %rows_hbm.1, s32[2,64]{1,0:T(2,128)} %bitcast.6, f32[2,64]{1,0:T(2,128)} %bitcast.7, bf16[1,6144,256]{2,1,0:T(8,128)(2,1)} %wg_hbm.1, bf16[1,6144,256]{2,1,0:T(8,128)(2,1)} %wu_hbm.1, bf16[1,256,6144]{2,1,0:T(8,128)(2,1)} %wd_hbm.1), custom_call_target="tpu_custom_call" | custom-call | tf_op jit(solution)/shard_map/pallas_call | solution.py:452
  96.4 2.1 %copy.8 = bf16[1,64,6144]{2,1,0:T(8,128)(2,1)} copy(bf16[1,64,6144]{2,1,0:T(8,128)(2,1)} %shard_map.64) | data formatting | bytes 1572864

commit v2 on v1

v2 whole, which is shorter than its diff:
```python
import functools

import jax
import jax.numpy as jnp
from jax import lax
from jax.experimental import pallas as pl
from jax.experimental.pallas import tpu as pltpu
from jax.sharding import PartitionSpec as P

F32 = jnp.float32
BF16 = jnp.bfloat16
MAIN = 16
EXTRA = 2
FOLD = MAIN // EXTRA
LANES = 256
MESH = pl.DeviceIdType.MESH


class Chunk:
    def __init__(self, pair, folded, start, width, turn, offset):
        self.pair = pair
        self.folded = folded
        self.cols = pl.ds(start, width)
        self.start = start
        self.width = width
        self.turn = turn
        self.room = pl.ds(offset, width)


GATHER = (2, 4, True)
REDUCE = (3, 4, False)
LAG = 1


def plan(depth, mains, shared, paired):
    unit = depth // FOLD
    singles, pairs = [], []
    thin = wide = at = 0
    if paired:
        pairs.append(Chunk(True, True, 0, unit, 1, 0))
        wide += unit
    else:
        singles.append(Chunk(False, True, 0, unit, 1, 0))
        thin += unit
    for i in range(mains):
        singles.append(Chunk(False, False, at, unit, -1 if i % 2 == 0 else 1, thin))
        at += unit
        thin += unit
    lines = (depth - at) // LANES
    for i in range(shared):
        width = (lines // shared + (1 if i < lines % shared else 0)) * LANES
        turn = 1 if (i + paired) % 2 == 0 else -1
        pairs.append(Chunk(True, False, at, width, turn, wide))
        at += width
        wide += width
    return singles, pairs


def iota(shape, dim):
    return lax.broadcasted_iota(jnp.int32, shape, dim)


def dot(a, b):
    return jnp.dot(a, b, preferred_element_type=F32)


def kernel(
    gather_plan,
    reduce_plan,
    rings,
    rows_hbm,
    ids_ref,
    probs_ref,
    wg_hbm,
    wu_hbm,
    wd_hbm,
    rows_p,
    eo_p,
    eot_p,
    meta_p,
    rows_v,
    wg,
    wu,
    wd,
    xg,
    xt,
    gacc,
    uacc,
    hid,
    part,
    pt,
    ring_pair,
    ring_one,
    cross_one,
    ends_s,
    eot_s,
    meta_s,
    send_sem,
    recv_sem,
    local_sem,
):
    singles, pairs = gather_plan
    tok, depth = rows_v.shape
    units = wg.shape[2]
    fold = depth // FOLD
    total = gacc.shape[0]
    section = lax.axis_index("section")
    sections = lax.axis_size("section")
    me = lax.axis_index("shard")
    core = lax.rem(me, 2)
    y = lax.rem(me // 2, 2)
    z = me // 4
    other = 1 - y

    def at_z(step):
        return lax.rem(z + step + rings, rings)

    def shard_of(zz, yy, cc):
        return {"shard": zz * 4 + yy * 2 + cc}

    following = {"section": lax.rem(section + 1, sections)}
    previous = {"section": lax.rem(section + sections - 1, sections)}
    across = shard_of(z, other, core)
    beside = {**following, **across}
    behind = {**previous, **across}
    sibling = shard_of(z, y, 1 - core)
    up_z = shard_of(at_z(1), y, core)
    down_z = shard_of(at_z(-1), y, core)
    far = rings // 2
    hops = {1: far, -1: far - 1}

    used = []
    started = []

    def remote(src, dst, device):
        i = len(used)
        used.append(i)
        copy = pltpu.make_async_remote_copy(
            src_ref=src,
            dst_ref=dst,
            send_sem=send_sem.at[i],
            recv_sem=recv_sem.at[i],
            device_id=device,
            device_id_type=MESH,
        )
        copy.start()
        started.append(copy)
        return copy

    rows_in = pltpu.make_async_copy(rows_hbm.at[0], rows_v, local_sem.at[0])
    rows_in.start()
    own = [
        pltpu.make_async_copy(wg_hbm.at[0], wg.at[0], local_sem.at[1]),
        pltpu.make_async_copy(wu_hbm.at[0], wu.at[0], local_sem.at[2]),
        pltpu.make_async_copy(wd_hbm.at[0], wd.at[pl.ds(0, units)], local_sem.at[3]),
    ]
    for copy in own:
        copy.start()

    barrier = pltpu.get_barrier_semaphore()
    for device in (up_z, down_z, across, sibling, previous, behind):
        pl.semaphore_signal(barrier, inc=1, device_id=device, device_id_type=MESH)

    hit = ids_ref[...] == section
    routed = jnp.max(jnp.where(hit, 1.0, 0.0).astype(F32), axis=0, keepdims=True)
    weight = jnp.sum(jnp.where(hit, probs_ref[...], 0.0), axis=0, keepdims=True)
    upper = (iota((tok, tok), 0) <= iota((tok, tok), 1)).astype(F32)
    count = dot(jnp.broadcast_to(routed, (8, tok)).astype(BF16), upper.astype(BF16))
    slot = jnp.where(routed > 0, count[0:1] - 1.0, -1.0)
    meta_s[...] = jnp.zeros_like(meta_s)
    meta_s[0:1, 0:tok] = slot
    meta_s[1:2, 0:tok] = weight
    place = iota((MAIN, tok), 0).astype(F32)
    placed = jnp.where(slot == place, 1.0, 0.0).astype(BF16)
    row16 = iota((MAIN, tok), 0)
    row_of = (MAIN + row16 // FOLD).astype(F32)

    def gathered(chunk):
        return xt if chunk.folded else xg

    rows_in.wait()
    for chunk in singles + pairs:
        if chunk.folded:
            folded = jnp.zeros((MAIN, fold), F32)
            for b in range(FOLD):
                pick = jnp.where((slot == row_of) & (row16 % FOLD == b), 1.0, 0.0)
                folded += dot(pick.astype(BF16), rows_v[:, b * fold : (b + 1) * fold])
            xt[y, z] = folded.astype(BF16)
        else:
            xg[y, z, :, chunk.cols] = dot(placed, rows_v[:, chunk.cols]).astype(BF16)

    pl.semaphore_wait(barrier, 6)
    weights = [
        remote(wg_hbm.at[0], wg.at[1], sibling),
        remote(wu_hbm.at[0], wu.at[1], sibling),
        remote(wd_hbm.at[0], wd.at[pl.ds(units, units)], sibling),
    ]

    ring = {}
    cross = {}

    def send_ring(chunk, hop, planes=None):
        ref = gathered(chunk)
        for turn in (chunk.turn, -chunk.turn):
            if hop > hops[turn * chunk.turn]:
                continue
            held = at_z(-turn * (hop - 1))
            if planes is None:
                block = ref.at[:, held, :, chunk.cols]
            else:
                block = ref.at[planes, held, :, chunk.cols]
            copy = remote(block, block, up_z if turn == 1 else down_z)
            ring.setdefault((chunk, turn, hop), []).append(copy)

    def await_ring(chunk, turn, hop):
        for copy in ring[chunk, turn, hop]:
            copy.wait_recv()

    def send_across(chunk, held, key):
        block = gathered(chunk).at[y, held, :, chunk.cols]
        cross[chunk, key] = remote(block, block, across)

    def advance(chunk, hop):
        for turn in (chunk.turn, -chunk.turn):
            if hop > hops[turn * chunk.turn]:
                continue
            await_ring(chunk, turn, hop)
            if not chunk.pair:
                send_across(chunk, at_z(-turn * hop), turn * hop)
        if hop < far:
            send_ring(chunk, hop + 1, None if chunk.pair else y)

    for chunk in singles:
        send_ring(chunk, 1, y)
    for chunk in pairs:
        send_across(chunk, z, 0)
        send_ring(chunk, 1, y)
    for chunk in singles:
        send_across(chunk, z, 0)
    for chunk in pairs:
        cross[chunk, 0].wait_recv()
        send_ring(chunk, 1, other)
    handed = [
        remote(rows_v, rows_p, following),
        remote(meta_s, meta_p, following),
    ]
    for hop in range(1, far):
        for chunk in singles:
            advance(chunk, hop)
        for chunk in pairs:
            advance(chunk, hop)

    for chunk in singles:
        advance(chunk, far)
    for copy in own[:2]:
        copy.wait()
    for copy in weights[:2]:
        copy.wait_recv()

    def await_single(chunk):
        for key in list(cross):
            if key[0] is chunk:
                cross[key].wait_recv()

    written = []

    def products(chunk):
        if chunk.pair:
            await_ring(chunk, chunk.turn, far)
        else:
            await_single(chunk)
        if chunk.folded:
            tail_rows()
            return
        for i in range(2):
            to = pl.ds(i * units, units)
            for acc, w in ((gacc, wg), (uacc, wu)):
                x = xg[:, :, :, chunk.cols].reshape(total, chunk.width)
                made = dot(x, w[i, chunk.cols, :])
                if written:
                    acc[:, to] += made
                else:
                    acc[:, to] = made
        written.append(chunk)

    def tail_rows():
        lane = iota((MAIN, rings * MAIN), 1)
        line = iota((MAIN, rings * MAIN), 0)
        home = (line // EXTRA) * MAIN + (line % EXTRA) * FOLD
        for yy in range(2):
            block = xt[yy].reshape(rings * MAIN, fold)
            for b in range(FOLD):
                pick = jnp.where(lane == home + b, 1.0, 0.0).astype(BF16)
                to = pl.ds(b * fold, fold)
                xg[yy, rings, :, to] = dot(pick, block).astype(BF16)

    folded_first = [c for c in singles + pairs if c.folded]
    mains_of = [c for c in singles if not c.folded]
    for chunk in folded_first + [c for c in pairs if not c.folded] + mains_of:
        products(chunk)

    rows_at_once = 2 * MAIN
    for r in range(0, total, rows_at_once):
        g = gacc[r : r + rows_at_once, :]
        u = uacc[r : r + rows_at_once, :]
        hid[r : r + rows_at_once, :] = (g / (1.0 + jnp.exp(-g)) * u).astype(BF16)

    singles, pairs = reduce_plan
    own[2].wait()
    weights[2].wait_recv()

    def down(chunk):
        step = 256
        for c in range(chunk.start, chunk.start + chunk.width, step):
            c1 = min(c + step, chunk.start + chunk.width)
            made = dot(hid[...], wd[:, c:c1]).astype(BF16)
            part[:, :, :, c:c1] = made.reshape(2, rings + 1, MAIN, c1 - c)

    def partial(chunk):
        return pt if chunk.folded else part

    sums = {}

    def slots(chunk):
        return ring_pair if chunk.pair else ring_one

    def index_of(chunk, turn, hop):
        return hop - 1 if turn == chunk.turn else far + hop - 1

    def send_sum(chunk, hop):
        ref = partial(chunk)
        for turn in (chunk.turn, -chunk.turn):
            last = hops[turn * chunk.turn]
            if hop > last:
                continue
            goal = at_z(turn * (last - hop + 1))
            i = index_of(chunk, turn, hop)
            if chunk.pair:
                src = ref.at[:, goal, :, chunk.cols]
                if hop > 1:
                    before = slots(chunk)[i - 1, :, :, chunk.room]
                    mine = ref[:, goal, :, chunk.cols]
                    ref[:, goal, :, chunk.cols] = (
                        mine.astype(F32) + before.astype(F32)
                    ).astype(BF16)
                dst = slots(chunk).at[i, :, :, chunk.room]
            else:
                src = ref.at[y, goal, :, chunk.cols]
                take_cross(chunk, turn * (last - hop + 1))
                if hop > 1:
                    before = slots(chunk)[i - 1, :, chunk.room]
                    mine = ref[y, goal, :, chunk.cols]
                    ref[y, goal, :, chunk.cols] = (
                        mine.astype(F32) + before.astype(F32)
                    ).astype(BF16)
                dst = slots(chunk).at[i, :, chunk.room]
            sums[chunk, turn, hop] = remote(src, dst, up_z if turn == 1 else down_z)

    crossed = {}

    def cross_single(chunk):
        for hop in range(1, far + 1):
            for turn in (chunk.turn, -chunk.turn):
                last = hops[turn * chunk.turn]
                if hop > last:
                    continue
                goal = at_z(turn * (last - hop + 1))
                block = partial(chunk).at[other, goal, :, chunk.cols]
                to = cross_one.at[goal, :, chunk.room]
                crossed[chunk, turn * (last - hop + 1)] = remote(block, to, across)
        block = partial(chunk).at[other, z, :, chunk.cols]
        crossed[chunk, 0] = remote(block, cross_one.at[z, :, chunk.room], across)

    def take_cross(chunk, step):
        crossed[chunk, step].wait_recv()
        ref, goal = partial(chunk), at_z(step)
        ref[y, goal, :, chunk.cols] = (
            ref[y, goal, :, chunk.cols].astype(F32)
            + cross_one[goal, :, chunk.room].astype(F32)
        ).astype(BF16)

    ones = singles[1:] + singles[:1]
    down(pairs[0])
    send_sum(pairs[0], 1)
    for chunk in singles[1:]:
        down(chunk)
        cross_single(chunk)
    for chunk in pairs[1:]:
        down(chunk)
        send_sum(chunk, 1)
    spot = iota((rings * MAIN, MAIN), 0)
    line = iota((rings * MAIN, MAIN), 1)
    home = (line // EXTRA) * MAIN + (line % EXTRA) * FOLD
    for yy in range(2):
        block = jnp.zeros((rings * MAIN, fold), F32)
        for b in range(FOLD):
            pick = jnp.where(spot == home + b, 1.0, 0.0).astype(BF16)
            block += dot(pick, part[yy, rings, :, b * fold : (b + 1) * fold])
        pt[yy] = block.astype(BF16).reshape(rings, MAIN, fold)
    cross_single(singles[0])

    def add(chunk, hop):
        for turn in (chunk.turn, -chunk.turn):
            if 1 < hop <= hops[turn * chunk.turn]:
                sums[chunk, turn, hop - 1].wait_recv()
        send_sum(chunk, hop)

    arrive = []

    def finish(chunk):
        for turn in (chunk.turn, -chunk.turn):
            sums[chunk, turn, hops[turn * chunk.turn]].wait_recv()
        ends = [
            index_of(chunk, chunk.turn, hops[1]),
            index_of(chunk, -chunk.turn, hops[-1]),
        ]
        return ends

    def finish_pair(chunk):
        ends = finish(chunk)
        for i, plane, device in ((1, other, beside), (0, y, following)):
            made = part[plane, z, :, chunk.cols].astype(F32)
            for end in ends:
                made += ring_pair[end, plane, :, chunk.room].astype(F32)
            ends_s[i, :, chunk.cols] = made.astype(BF16)
            block = ends_s.at[i, :, chunk.cols]
            arrive.append(remote(block, eo_p.at[i, :, chunk.cols], device))

    def finish_one(chunk):
        take_cross(chunk, 0)
        ends = finish(chunk)
        made = partial(chunk)[y, z, :, chunk.cols].astype(F32)
        for end in ends:
            made += ring_one[end, :, chunk.room].astype(F32)
        if chunk.folded:
            eot_s[...] = made.astype(BF16)
            arrive.append(remote(eot_s, eot_p, following))
        else:
            ends_s[0, :, chunk.cols] = made.astype(BF16)
            block = ends_s.at[0, :, chunk.cols]
            arrive.append(remote(block, eo_p.at[0, :, chunk.cols], following))

    for step in range(2, far + LAG + 2):
        behind_by = step - LAG
        for chunk in pairs:
            if step <= far:
                add(chunk, step)
            elif step == far + 1:
                finish_pair(chunk)
        for chunk in ones:
            if 1 <= behind_by <= far:
                add(chunk, behind_by)
            elif behind_by == far + 1:
                finish_one(chunk)

    for copy in handed + arrive:
        copy.wait_recv()
    for copy in started:
        copy.wait_send()
    assert len(used) == send_sem.shape[0]


def combine(singles, pairs, rows_p, eo_p, eot_p, meta_p, out_ref, made, done):
    tok, depth = rows_p.shape
    fold = depth // FOLD
    diagonal = iota((tok, tok), 0) == iota((tok, tok), 1)

    def upright(i):
        line = jnp.broadcast_to(meta_p[i : i + 1, 0:tok], (tok, tok))
        return jnp.sum(jnp.where(diagonal, line, 0.0), axis=1, keepdims=True)

    slot_p = upright(0)
    weight_p = upright(1)
    spot = iota((tok, MAIN), 1)
    taken = jnp.where(slot_p == spot.astype(F32), 1.0, 0.0).astype(BF16)
    extra_of = (MAIN + spot // FOLD).astype(F32)
    copies = []
    for b in range(FOLD):
        at = pl.ds(b * fold, fold)
        pick = jnp.where((slot_p == extra_of) & (spot % FOLD == b), 1.0, 0.0)
        added = dot(taken, eo_p[0, :, at]) + dot(pick.astype(BF16), eot_p[...])
        if b * fold >= pairs[0].start:
            added += dot(taken, eo_p[1, :, at])
        made[:, at] = (rows_p[:, at].astype(F32) + weight_p * added).astype(BF16)
        copies.append(pltpu.make_async_copy(made.at[:, at], out_ref.at[0, :, at], done.at[b]))
        copies[-1].start()
    for copy in copies:
        copy.wait()


def on_device(rows, expert_ids, gate_probs, w_gate, w_up, w_down):
    _, tok, depth = rows.shape
    units = w_gate.shape[2]
    rings = lax.axis_size("shard") // 4
    gather_plan, reduce_plan = plan(depth, *GATHER), plan(depth, *REDUCE)
    singles, pairs = gather_plan
    fold = depth // FOLD
    total = 2 * (rings + 1) * MAIN
    steps = rings - 1
    copies = 5
    copies += len(singles) * (steps + rings) + len(pairs) * (steps + 3)
    singles, pairs = reduce_plan
    copies += len(singles) * (steps + rings) + len(pairs) * steps
    copies += len(singles) + 2 * len(pairs)
    wide = sum(c.width for c in pairs)
    thin = sum(c.width for c in singles)
    ids = jnp.transpose(expert_ids[0])
    probs = jnp.transpose(gate_probs[0])
    hbm = pl.BlockSpec(memory_space=pltpu.MemorySpace.HBM)
    vmem = pl.BlockSpec(memory_space=pltpu.MemorySpace.VMEM)
    handed = pl.pallas_call(
        functools.partial(kernel, gather_plan, reduce_plan, rings),
        out_shape=[
            pltpu.VMEM((tok, depth), BF16),
            pltpu.VMEM((2, MAIN, depth), BF16),
            pltpu.VMEM((MAIN, fold), BF16),
            pltpu.VMEM((8, 128), F32),
        ],
        in_specs=[hbm, vmem, vmem, hbm, hbm, hbm],
        out_specs=[vmem] * 4,
        scratch_shapes=[
            pltpu.VMEM((tok, depth), BF16),
            pltpu.VMEM((2, depth, units), BF16),
            pltpu.VMEM((2, depth, units), BF16),
            pltpu.VMEM((2 * units, depth), BF16),
            pltpu.VMEM((2, rings + 1, MAIN, depth), BF16),
            pltpu.VMEM((2, rings, MAIN, fold), BF16),
            pltpu.VMEM((total, 2 * units), F32),
            pltpu.VMEM((total, 2 * units), F32),
            pltpu.VMEM((total, 2 * units), BF16),
            pltpu.VMEM((2, rings + 1, MAIN, depth), BF16),
            pltpu.VMEM((2, rings, MAIN, fold), BF16),
            pltpu.VMEM((steps, 2, MAIN, wide), BF16),
            pltpu.VMEM((steps, MAIN, thin), BF16),
            pltpu.VMEM((rings, MAIN, thin), BF16),
            pltpu.VMEM((2, MAIN, depth), BF16),
            pltpu.VMEM((MAIN, fold), BF16),
            pltpu.VMEM((8, 128), F32),
            pltpu.SemaphoreType.DMA((copies,)),
            pltpu.SemaphoreType.DMA((copies,)),
            pltpu.SemaphoreType.DMA((4,)),
        ],
        compiler_params=pltpu.CompilerParams(
            collective_id=0, has_side_effects=True, vmem_limit_bytes=58 << 20
        ),
    )(rows, ids, probs, w_gate, w_up, w_down)
    return pl.pallas_call(
        functools.partial(combine, singles, pairs),
        out_shape=jax.ShapeDtypeStruct(rows.shape, BF16),
        in_specs=[vmem] * 4,
        out_specs=hbm,
        scratch_shapes=[
            pltpu.VMEM((tok, depth), BF16),
            pltpu.SemaphoreType.DMA((FOLD,)),
        ],
        compiler_params=pltpu.CompilerParams(vmem_limit_bytes=8 << 20),
    )(*handed)


def solution(mesh):
    in_specs = (
        P("section", "shard", None),
        P("section", "shard", None),
        P("section", "shard", None),
        P("section", None, "shard"),
        P("section", None, "shard"),
        P("section", "shard", None),
    )
    out_specs = P("section", "shard", None)
    return jax.shard_map(
        on_device, mesh=mesh, in_specs=in_specs, out_specs=out_specs, check_vma=False
    )
```

time: 98.6 us -> 85.9 us (0.87)
  the two profiles are of different devices: /device:TPU:8 before, /device:TPU:40 now
where the time goes in v2:
time: 85.9 us; the launch traced here: 84.3 us
  Pallas kernels  84.3 us (98%)
    pallas_call x1, Pallas kernels, on_device(): pl.pallas_call(functools.partial(kernel, gather_plan, reduce_plan, rings)...  82.9 us

profile of v2, /device:TPU:40, one launch (start us, length us, event | category | flops | bytes accessed | tf_op | source)
XLA Modules:
  0.0 84.3 jit_solution(14759536594269480333)
XLA Ops:
  0.0 82.9 %shard_map.64 = (bf16[64,6144]{1,0:T(8,128)(2,1)S(1)}, bf16[2,16,6144]{2,1,0:T(8,128)(2,1)S(1)}, bf16[16,768]{1,0:T(8,128)(2,1)S(1)}, f32[8,128]{1,0:T(8,128)S(1)}) custom-call(bf16[1,64,6144]{2,1,0:T(8,128)(2,1)} %rows_hbm.1, s32[2,64]{1,0:T(2,128)} %bitcast.6, f32[2,64]{1,0:T(2,128)} %bitcast.7, bf16[1,6144,256]{2,1,0:T(8,128)(2,1)} %wg_hbm.1, ...), custom_call_target="tpu_custom_call" | custom-call | tf_op jit(solution)/shard_map/pallas_call | solution.py:511
  82.9 1.5 %shard_map.65 = bf16[1,64,6144]{2,1,0:T(8,128)(2,1)} custom-call(bf16[64,6144]{1,0:T(8,128)(2,1)S(1)} %get-tuple-element.9.rows_p, bf16[2,16,6144]{2,1,0:T(8,128)(2,1)S(1)} %get-tuple-element.10.eo_p, bf16[16,768]{1,0:T(8,128)(2,1)S(1)} %get-tuple-element.11.eot_p, f32[8,128]{1,0:T(8,128)S(1)} %get-tuple-element.12.meta_p), custom_call_target="tpu_custom_call" | custom-call | tf_op jit(solution)/shard_map/pallas_call | solution.py:547

commit v3 on v2

--- a/solution.py
+++ b/solution.py
@@ -28,31 +28,34 @@
 
 
 GATHER = (2, 4, True)
-REDUCE = (3, 4, False)
+REDUCE = (4, 4, False)
 LAG = 1
 
 
 def plan(depth, mains, shared, paired):
     unit = depth // FOLD
     singles, pairs = [], []
-    thin = wide = at = 0
+    lines = (depth - mains * unit) // LANES
+    load = {1: 0, -1: 0}
+    held = {True: 0, False: 0}
+
+    def make(pair, folded, start, width):
+        turn = 1 if load[1] <= load[-1] else -1
+        load[turn] += width * (2 if pair else 1)
+        (pairs if pair else singles).append(Chunk(pair, folded, start, width, turn, held[pair]))
+        held[pair] += width
+
     if paired:
-        pairs.append(Chunk(True, True, 0, unit, 1, 0))
-        wide += unit
-    else:
-        singles.append(Chunk(False, True, 0, unit, 1, 0))
-        thin += unit
-    for i in range(mains):
-        singles.append(Chunk(False, False, at, unit, -1 if i % 2 == 0 else 1, thin))
-        at += unit
-        thin += unit
-    lines = (depth - at) // LANES
+        make(True, True, 0, unit)
+    at = mains * unit
     for i in range(shared):
         width = (lines // shared + (1 if i < lines % shared else 0)) * LANES
-        turn = 1 if (i + paired) % 2 == 0 else -1
-        pairs.append(Chunk(True, False, at, width, turn, wide))
+        make(True, False, at, width)
         at += width
-        wide += width
+    if not paired:
+        make(False, True, 0, unit)
+    for i in range(mains):
+        make(False, False, i * unit, unit)
     return singles, pairs
 
 
@@ -358,18 +361,17 @@
 
     crossed = {}
 
-    def cross_single(chunk):
-        for hop in range(1, far + 1):
-            for turn in (chunk.turn, -chunk.turn):
-                last = hops[turn * chunk.turn]
-                if hop > last:
-                    continue
-                goal = at_z(turn * (last - hop + 1))
-                block = partial(chunk).at[other, goal, :, chunk.cols]
-                to = cross_one.at[goal, :, chunk.room]
-                crossed[chunk, turn * (last - hop + 1)] = remote(block, to, across)
-        block = partial(chunk).at[other, z, :, chunk.cols]
-        crossed[chunk, 0] = remote(block, cross_one.at[z, :, chunk.room], across)
+    def cross_single(chunk, hop):
+        steps = []
+        for turn in (chunk.turn, -chunk.turn):
+            last = hops[turn * chunk.turn]
+            if hop <= last:
+                steps.append(turn * (last - hop + 1))
+        for step in steps or [0]:
+            goal = at_z(step)
+            block = partial(chunk).at[other, goal, :, chunk.cols]
+            to = cross_one.at[goal, :, chunk.room]
+            crossed[chunk, step] = remote(block, to, across)
 
     def take_cross(chunk, step):
         crossed[chunk, step].wait_recv()
@@ -384,7 +386,7 @@
     send_sum(pairs[0], 1)
     for chunk in singles[1:]:
         down(chunk)
-        cross_single(chunk)
+        cross_single(chunk, 1)
     for chunk in pairs[1:]:
         down(chunk)
         send_sum(chunk, 1)
@@ -397,7 +399,10 @@
             pick = jnp.where(spot == home + b, 1.0, 0.0).astype(BF16)
             block += dot(pick, part[yy, rings, :, b * fold : (b + 1) * fold])
         pt[yy] = block.astype(BF16).reshape(rings, MAIN, fold)
-    cross_single(singles[0])
+    cross_single(singles[0], 1)
+    for hop in range(2, far + 2):
+        for chunk in ones:
+            cross_single(chunk, hop)
 
     def add(chunk, hop):
         for turn in (chunk.turn, -chunk.turn):

time: 85.9 us -> 83.1 us (0.967)
  Pallas kernels: 84.3 us -> 82.1 us
    pallas_call x1, Pallas kernels: 82.9 us -> 80.6 us  [on_device(): pl.pallas_call(functools.partial(kernel, gather_plan, reduce_plan, rings)...]
where the time goes in v3:
time: 83.1 us; the launch traced here: 82.1 us
  Pallas kernels  82.1 us (99%)
    pallas_call x1, Pallas kernels, on_device(): pl.pallas_call(functools.partial(kernel, gather_plan, reduce_plan, rings)...  80.6 us

profile of v3, /device:TPU:40, one launch (start us, length us, event | category | flops | bytes accessed | tf_op | source)
XLA Modules:
  0.0 82.1 jit_solution(3994447873590150099)
XLA Ops:
  0.0 80.6 %shard_map.64 = (bf16[64,6144]{1,0:T(8,128)(2,1)S(1)}, bf16[2,16,6144]{2,1,0:T(8,128)(2,1)S(1)}, bf16[16,768]{1,0:T(8,128)(2,1)S(1)}, f32[8,128]{1,0:T(8,128)S(1)}) custom-call(bf16[1,64,6144]{2,1,0:T(8,128)(2,1)} %rows_hbm.1, s32[2,64]{1,0:T(2,128)} %bitcast.6, f32[2,64]{1,0:T(2,128)} %bitcast.7, bf16[1,6144,256]{2,1,0:T(8,128)(2,1)} %wg_hbm.1, ...), custom_call_target="tpu_custom_call" | custom-call | tf_op jit(solution)/shard_map/pallas_call | solution.py:516
  80.6 1.5 %shard_map.65 = bf16[1,64,6144]{2,1,0:T(8,128)(2,1)} custom-call(bf16[64,6144]{1,0:T(8,128)(2,1)S(1)} %get-tuple-element.9.rows_p, bf16[2,16,6144]{2,1,0:T(8,128)(2,1)S(1)} %get-tuple-element.10.eo_p, bf16[16,768]{1,0:T(8,128)(2,1)S(1)} %get-tuple-element.11.eot_p, f32[8,128]{1,0:T(8,128)S(1)} %get-tuple-element.12.meta_p), custom_call_target="tpu_custom_call" | custom-call | tf_op jit(solution)/shard_map/pallas_call | solution.py:552
